TPU v7x, 512 devices: a whole 4x4x16 slice. The times are simulated.
512 devices in a mesh: dp: 128 (over z, x, core), mp: 4 (over y).
Axes of the slice: x: 4, y: 4, z: 16, core: 2. Of those that a mesh axis runs over, the one named last changes fastest.
Arguments:
- session_length: int32 [128], P('dp'), may hold values from 1 to 128
- event_owner: int32 [16384, 1], P('dp'), may hold values from 0 to 127; in each aligned block of 128 rows (0 to 127, 128 to 255, ...) at most 2 rows name the same one
- event_row: int32 [16384], P('dp'), may hold values from 0 to 255
- text_rows: bfloat16 [32768, 4096], P('dp', 'mp'), may hold values from -6 to 6
- image_rows: bfloat16 [32768, 4096], P('dp', 'mp'), may hold values from -6 to 6
- price: float32 [32768], P('dp'), may hold values from 0.2 to 5
- price_dir: bfloat16 [4096], P('mp'), may hold values from -4 to 4
- norm_gain: bfloat16 [4096], P('mp'), may hold values from 0.5 to 1.5
- w_query: bfloat16 [4096, 2048], P('dp', 'mp'), may hold values from -1 to 1
- w_key: bfloat16 [4096, 2048], P('dp', 'mp'), may hold values from -1 to 1
- w_value: bfloat16 [4096, 2048], P('dp', 'mp'), may hold values from -0.09375 to 0.09375
- cotangent: bfloat16 [16384, 4096], P('dp', 'mp'), may hold values from -6 to 6
Outputs:
- context: bfloat16 [16384, 2048], P('dp', 'mp')
- text_grad: float32 [32768, 4096], P('dp', 'mp')
- image_grad: float32 [32768, 4096], P('dp', 'mp')
Inputs may be any that keep to these rules, and one draw needn't show every extreme that they name: `event_owner`: among the event slots of one index of dp, no owner is named more than 2 times, a bound that some block reaches.
All inputs are finite; a program needn't handle non-finite values.
Results may differ from a plain program's by a relative error of at most 0.0063.
Values may be sent and summed in bfloat16 or wider, within the bound.
No kernel may reach another device: no remote copies, remote signals or barrier semaphores. Data moves between devices by JAX's collectives and lax.ppermute only.
A program may use at most 64 MiB of HBM per device.

v0:
```python
import math
import jax
import jax.numpy as jnp
from jax import lax
from jax.sharding import PartitionSpec as P

HD = 128
SLOT = 128


def one_hot(rows, columns):
    return (rows[:, None] == columns[None, :]).astype(jnp.bfloat16)


def pick(selector, values):
    return jnp.dot(selector, values, preferred_element_type=jnp.float32)


def attend(query, keys, values, session_length):
    heads_here = query.shape[1] // HD
    shape3 = (SLOT, heads_here, HD)
    scores = jnp.einsum(
        "qhd,khd->hqk",
        query.reshape(shape3),
        keys.reshape(shape3),
        preferred_element_type=jnp.float32,
    ) / math.sqrt(HD)
    position = jnp.arange(SLOT, dtype=jnp.int32)
    live_mask = position < session_length[0]
    allowed = (position[None, :] <= position[:, None])[None] & live_mask[None, None, :]
    scores = jnp.where(allowed, scores, jnp.float32(-1e30))
    row_max = jnp.max(scores, axis=-1, keepdims=True)
    powers = jnp.exp(scores - row_max)
    probs = (powers / jnp.sum(powers, axis=-1, keepdims=True)).astype(jnp.bfloat16)
    context = jnp.einsum(
        "hqk,khd->qhd", probs, values.reshape(shape3), preferred_element_type=jnp.float32
    )
    context = jnp.where(live_mask[:, None, None], context, jnp.float32(0.0))
    return context.reshape(SLOT, heads_here * HD).astype(jnp.bfloat16)


def local(
    session_length,
    event_owner,
    event_row,
    text_rows,
    image_rows,
    price,
    price_dir,
    norm_gain,
    w_query,
    w_key,
    w_value,
    cotangent,
):
    peers = lax.axis_size("dp")
    parts = lax.axis_size("mp")
    mine = lax.axis_index("mp")
    tok_count = event_row.shape[0]
    capacity = 2 * tok_count // peers
    col_width = text_rows.shape[1]
    table_rows = text_rows.shape[0]
    slots = jnp.arange(peers * capacity, dtype=jnp.int32)
    weights = lax.all_gather(
        jnp.concatenate([w_query, w_key, w_value], axis=1), "dp", axis=0, tiled=True
    )
    owner_ids = event_owner[:, 0]
    place = jnp.arange(tok_count, dtype=jnp.int32)
    same = (owner_ids[:, None] == owner_ids[None, :]) & (place[None, :] < place[:, None])
    slot_ids = owner_ids * capacity + jnp.sum(same.astype(jnp.int32), axis=1)
    taken = slots[:, None] == slot_ids[None, :]
    requests = (jnp.sum(jnp.where(taken, event_row[None, :] + 1, 0), axis=1) - 1).reshape(
        peers, capacity
    )
    got_ids = lax.all_to_all(requests, "dp", split_axis=0, concat_axis=0, tiled=True).reshape(-1)
    text_float = text_rows.astype(jnp.float32)
    image_float = image_rows.astype(jnp.float32)
    table = (
        text_float * image_float + price[:, None] * price_dir.astype(jnp.float32)[None, :]
    ).astype(jnp.bfloat16)
    wanted = one_hot(got_ids, jnp.arange(table_rows, dtype=jnp.int32))
    replies = lax.all_to_all(
        pick(wanted, table).astype(jnp.bfloat16).reshape(peers, capacity, col_width),
        "dp",
        split_axis=0,
        concat_axis=0,
        tiled=True,
    ).reshape(peers * capacity, col_width)
    grad_buffer = pick(taken.astype(jnp.bfloat16), cotangent).astype(jnp.bfloat16)
    grad_buffer, replies = lax.optimization_barrier((grad_buffer, replies))
    got_grads = lax.all_to_all(
        grad_buffer.reshape(peers, capacity, col_width),
        "dp",
        split_axis=0,
        concat_axis=0,
        tiled=True,
    ).reshape(peers * capacity, col_width)
    row_sums = pick(wanted.T, got_grads)
    text_grad = row_sums * image_float
    image_grad = row_sums * text_float
    joined = pick(one_hot(slot_ids, slots), replies).astype(jnp.bfloat16)
    turns = [
        (
            joined
            if k == 0
            else lax.ppermute(joined, "mp", [(i, (i + k) % parts) for i in range(parts)])
        )
        for k in range(parts)
    ]
    stacked = jnp.stack(turns)
    features = jnp.concatenate(
        [
            lax.dynamic_index_in_dim(stacked, (mine - s) % parts, 0, keepdims=False)
            for s in range(parts)
        ],
        axis=1,
    ).astype(jnp.float32)
    gain = lax.all_gather(norm_gain, "mp", axis=0, tiled=True).astype(jnp.float32)
    scale = lax.rsqrt(jnp.mean(features * features, axis=1, keepdims=True) + 1e-06)
    normed = (features * scale * gain[None, :]).astype(jnp.bfloat16)
    projected = jnp.dot(normed, weights, preferred_element_type=jnp.float32).astype(jnp.bfloat16)
    width = w_query.shape[1]
    context = attend(
        projected[:, :width],
        projected[:, width : 2 * width],
        projected[:, 2 * width :],
        session_length,
    )
    return (context, text_grad, image_grad)


def solution(mesh):
    return jax.shard_map(
        local,
        mesh=mesh,
        in_specs=(
            P("dp"),
            P("dp", None),
            P("dp"),
            P("dp", "mp"),
            P("dp", "mp"),
            P("dp"),
            P("mp"),
            P("mp"),
            P("dp", "mp"),
            P("dp", "mp"),
            P("dp", "mp"),
            P("dp", "mp"),
        ),
        out_specs=(P("dp", "mp"), P("dp", "mp"), P("dp", "mp")),
        check_vma=False,
    )
```

profile of v0, /device:TPU:1, one launch (start us, length us, event | category | flops | bytes accessed | tf_op | source)
XLA Modules:
  0.0 196.3 jit_solution(1731019495664114980)
XLA Ops:
  7.2 0.0 copy-start
  7.2 0.0 all-gather.2.cloned.1.call-start
  7.2 1.5 pad_maximum_fusion.3
  8.7 0.0 all-gather.2.cloned.1.call-update
  8.7 0.9 convert_reduce_fusion
  9.6 0.7 multiply_add_fusion
  10.3 0.1 select_reduce_fusion
  10.4 0.8 sub.24
  11.2 20.4 %all-to-all-start = ((s32[128,1,2]{2,1,0:T(1,128)}), s32[128,1,2]{2,1,0:T(1,128)S(1)}, u32[]{:S(2)}, u32[]{:S(2)}) async-start(s32[128,1,2]{2,1,0:T(1,128)} %bitcast.4), calls=%async_computation | async-start | bytes 131072 | tf_op jit(solution)/shard_map/all_to_all | solution.py:75
  31.6 0.7 convert_element_type.55
  32.3 14.1 %all-to-all-done = s32[128,1,2]{2,1,0:T(1,128)S(1)} async-done(((s32[128,1,2]{2,1,0:T(1,128)}), s32[128,1,2]{2,1,0:T(1,128)S(1)}, u32[]{:S(2)}, u32[]{:S(2)}) %all-to-all-start) | async-done | bytes 1056 | tf_op jit(solution)/shard_map/all_to_all | solution.py:75
  46.4 0.5 broadcast.75
  47.0 0.8 reduce.3
  47.8 0.1 eq.74
  47.9 1.7 convolution_convert_fusion.1
  49.6 1.0 reshape.110
  50.6 5.7 %all-to-all-start.1 = ((bf16[128,2,1024]{2,1,0:T(2,128)(2,1)}), bf16[128,2,1024]{2,1,0:T(2,128)(2,1)S(1)}, u32[]{:S(2)}, u32[]{:S(2)}) async-start(bf16[128,2,1024]{2,1,0:T(2,128)(2,1)} %reshape.110), calls=%async_computation.1 | async-start | bytes 1048576 | tf_op jit(solution)/shard_map/all_to_all | solution.py:82
  56.3 0.0 copy-done
  56.3 0.0 copy-start.4
  56.3 0.3 convolution_convert_fusion.2
  56.6 0.0 copy-start.3
  56.6 33.6 %all-to-all-done.1 = bf16[128,2,1024]{2,1,0:T(2,128)(2,1)S(1)} async-done(((bf16[128,2,1024]{2,1,0:T(2,128)(2,1)}), bf16[128,2,1024]{2,1,0:T(2,128)(2,1)S(1)}, u32[]{:S(2)}, u32[]{:S(2)}) %all-to-all-start.1) | async-done | bytes 524320 | tf_op jit(solution)/shard_map/all_to_all | solution.py:82
  90.2 0.2 reshape.111
  90.4 1.0 reshape.115
  91.3 9.5 %all-to-all-start.2 = ((bf16[128,2,1024]{2,1,0:T(2,128)(2,1)}), bf16[128,2,1024]{2,1,0:T(2,128)(2,1)S(1)}, u32[]{:S(2)}, u32[]{:S(2)}) async-start(bf16[128,2,1024]{2,1,0:T(2,128)(2,1)} %reshape.115), calls=%async_computation.2 | async-start | bytes 1048576 | tf_op jit(solution)/shard_map/all_to_all | solution.py:91
  101.5 0.0 copy-done.4
  101.6 0.3 convolution_convert_fusion.3
  101.8 3.2 %collective-permute-start = (bf16[128,1024]{1,0:T(8,128)(2,1)S(1)}, bf16[128,1024]{1,0:T(8,128)(2,1)S(1)}, u32[]{:S(2)}, u32[]{:S(2)}) collective-permute-start(bf16[128,1024]{1,0:T(8,128)(2,1)S(1)} %convolution_convert_fusion.3), channel_id=1, source_target_pairs={{0,1},{1,2},{2,3},{3,0},{4,5},{5,6},{6,7},{7,4},{8,9},{9,10},{10,1... | collective-permute-start | bytes 786440 | tf_op jit(solution)/shard_map/ppermute | solution.py:106
  105.0 4.4 %collective-permute-start.1 = (bf16[128,1024]{1,0:T(8,128)(2,1)S(1)}, bf16[128,1024]{1,0:T(8,128)(2,1)S(1)}, u32[]{:S(2)}, u32[]{:S(2)}) collective-permute-start(bf16[128,1024]{1,0:T(8,128)(2,1)S(1)} %convolution_convert_fusion.3), channel_id=1, source_target_pairs={{0,2},{1,3},{2,0},{3,1},{4,6},{5,7},{6,4},{7,5},{8,10},{9,11},{10,... | collective-permute-start | bytes 786440 | tf_op jit(solution)/shard_map/ppermute | solution.py:106
  109.4 3.0 %collective-permute-start.2 = (bf16[128,1024]{1,0:T(8,128)(2,1)S(1)}, bf16[128,1024]{1,0:T(8,128)(2,1)S(1)}, u32[]{:S(2)}, u32[]{:S(2)}) collective-permute-start(bf16[128,1024]{1,0:T(8,128)(2,1)S(1)} %convolution_convert_fusion.3), channel_id=1, source_target_pairs={{0,3},{1,0},{2,1},{3,2},{4,7},{5,4},{6,5},{7,6},{8,11},{9,8},{10,9... | collective-permute-start | bytes 786440 | tf_op jit(solution)/shard_map/ppermute | solution.py:106
  112.5 0.0 copy-done.3
  112.5 13.0 %all_gather.6 = bf16[4096]{0:T(1024)(128)(2,1)S(1)} all-gather(bf16[1024]{0:T(1024)(128)(2,1)S(1)} %copy-done.3), channel_id=1, replica_groups=mesh['dp'=128,'mp'=4] {'mp'}, dimensions={0}, use_global_device_ids=true | all-gather | bytes 10240 | tf_op jit(solution)/shard_map/all_gather | solution.py:118
  125.6 0.1 fusion.27
  125.7 0.0 collective-permute-done
  125.7 0.0 collective-permute-done.1
  125.7 0.0 collective-permute-done.2
  125.7 0.1 pad_maximum_fusion
  125.9 0.0 copy-start.1
  125.9 0.0 copy-start.2
  125.9 0.1 dynamic-slice_bitcast_fusion.3
  126.0 0.3 fusion.1
  126.3 7.7 %all-to-all-done.2 = bf16[128,2,1024]{2,1,0:T(2,128)(2,1)S(1)} async-done(((bf16[128,2,1024]{2,1,0:T(2,128)(2,1)}), bf16[128,2,1024]{2,1,0:T(2,128)(2,1)S(1)}, u32[]{:S(2)}, u32[]{:S(2)}) %all-to-all-start.2) | async-done | bytes 524320 | tf_op jit(solution)/shard_map/all_to_all | solution.py:91
  134.0 0.2 reshape.116
  134.2 0.0 copy-done.1
  134.2 0.0 copy-done.2
  134.3 1.7 convert_multiply_fusion.4
  136.0 45.6 %all-gather.2.cloned.1.call-done = bf16[4096,1536]{1,0:T(8,128)(2,1)} async-done(((bf16[32,1536]{1,0:T(8,128)(2,1)}), bf16[4096,1536]{1,0:T(8,128)(2,1)}) %all-gather.2.cloned.1.call-update) | async-done | bytes 12582928 | tf_op jit(solution)/shard_map/all_gather | solution.py:64
  181.6 6.4 %convolution_convert_fusion = bf16[128,1536]{1,0:T(8,128)(2,1)S(1)} fusion(bf16[4096,1536]{1,0:T(8,128)(2,1)} %all-gather.2.cloned.1.call-done, f32[4096]{0:T(1024)S(1)} %convert_element_type.60, f32[128]{0:T(128)S(1)} %add_rsqrt_fusion, bf16[128,1024]{1,0:T(8,128)(2,1)S(1)} %get-tuple-element.22, bf16[128,1024]{1,0:T(8,128)(2,1)S(1)} %get-tuple-element.23, ...), kind=kOutput, calls=%fused_computation.3 | convolution fusion | flops 1616576512 | bytes 14041600 | tf_op jit(solution)/shard_map/dot_general | solution.py:121
  188.0 0.2 fusion.5
  188.2 0.1 fusion.31
  188.3 0.1 copy.38
  188.4 0.2 fusion.7
  188.7 0.8 copy.36
  (6 shorter events, 0.1 us)
Async XLA Ops:
  7.2 49.1 %copy-start = (bf16[128,1024]{1,0:T(8,128)(2,1)S(1)}, bf16[128,1024]{1,0:T(8,128)(2,1)}, u32[]{:S(2)}) copy-start(bf16[128,1024]{1,0:T(8,128)(2,1)} %param.23) | copy-start | bytes 786436
  7.2 174.4 %all-gather.2.cloned.1.call-start = ((), (), s32[]{:S(2)}) async-start(), calls=%async_computation.3 | async-start | bytes 12681216 | tf_op jit(solution)/shard_map/all_gather | solution.py:64
  11.2 35.2 %all-to-all-start = ((s32[128,1,2]{2,1,0:T(1,128)}), s32[128,1,2]{2,1,0:T(1,128)S(1)}, u32[]{:S(2)}, u32[]{:S(2)}) async-start(s32[128,1,2]{2,1,0:T(1,128)} %bitcast.4), calls=%async_computation | async-start | bytes 131072 | tf_op jit(solution)/shard_map/all_to_all | solution.py:75
  50.6 39.6 %all-to-all-start.1 = ((bf16[128,2,1024]{2,1,0:T(2,128)(2,1)}), bf16[128,2,1024]{2,1,0:T(2,128)(2,1)S(1)}, u32[]{:S(2)}, u32[]{:S(2)}) async-start(bf16[128,2,1024]{2,1,0:T(2,128)(2,1)} %reshape.110), calls=%async_computation.1 | async-start | bytes 1048576 | tf_op jit(solution)/shard_map/all_to_all | solution.py:82
  56.3 45.3 %copy-start.4 = (s32[128,1]{0,1:T(1,128)S(1)}, s32[128,1]{0,1:T(1,128)}, u32[]{:S(2)}) copy-start(s32[128,1]{0,1:T(1,128)} %param.13) | copy-start | bytes 1540
  56.6 56.0 %copy-start.3 = (bf16[1024]{0:T(1024)(128)(2,1)S(1)}, bf16[1024]{0:T(1024)(128)(2,1)}, u32[]{:S(2)}) copy-start(bf16[1024]{0:T(1024)(128)(2,1)} %param.19) | copy-start | bytes 6148
  91.3 42.7 %all-to-all-start.2 = ((bf16[128,2,1024]{2,1,0:T(2,128)(2,1)}), bf16[128,2,1024]{2,1,0:T(2,128)(2,1)S(1)}, u32[]{:S(2)}, u32[]{:S(2)}) async-start(bf16[128,2,1024]{2,1,0:T(2,128)(2,1)} %reshape.115), calls=%async_computation.2 | async-start | bytes 1048576 | tf_op jit(solution)/shard_map/all_to_all | solution.py:91
  101.8 23.9 %collective-permute-start = (bf16[128,1024]{1,0:T(8,128)(2,1)S(1)}, bf16[128,1024]{1,0:T(8,128)(2,1)S(1)}, u32[]{:S(2)}, u32[]{:S(2)}) collective-permute-start(bf16[128,1024]{1,0:T(8,128)(2,1)S(1)} %convolution_convert_fusion.3), channel_id=1, source_target_pairs={{0,1},{1,2},{2,3},{3,0},{4,5},{5,6},{6,7},{7,4},{8,9},{9,10},{10,1... | collective-permute-start | bytes 786440 | tf_op jit(solution)/shard_map/ppermute | solution.py:106
  105.0 20.7 %collective-permute-start.1 = (bf16[128,1024]{1,0:T(8,128)(2,1)S(1)}, bf16[128,1024]{1,0:T(8,128)(2,1)S(1)}, u32[]{:S(2)}, u32[]{:S(2)}) collective-permute-start(bf16[128,1024]{1,0:T(8,128)(2,1)S(1)} %convolution_convert_fusion.3), channel_id=1, source_target_pairs={{0,2},{1,3},{2,0},{3,1},{4,6},{5,7},{6,4},{7,5},{8,10},{9,11},{10,... | collective-permute-start | bytes 786440 | tf_op jit(solution)/shard_map/ppermute | solution.py:106
  109.4 16.3 %collective-permute-start.2 = (bf16[128,1024]{1,0:T(8,128)(2,1)S(1)}, bf16[128,1024]{1,0:T(8,128)(2,1)S(1)}, u32[]{:S(2)}, u32[]{:S(2)}) collective-permute-start(bf16[128,1024]{1,0:T(8,128)(2,1)S(1)} %convolution_convert_fusion.3), channel_id=1, source_target_pairs={{0,3},{1,0},{2,1},{3,2},{4,7},{5,4},{6,5},{7,6},{8,11},{9,8},{10,9... | collective-permute-start | bytes 786440 | tf_op jit(solution)/shard_map/ppermute | solution.py:106
  125.9 8.4 %copy-start.1 = (bf16[256,1024]{1,0:T(8,128)(2,1)S(1)}, bf16[256,1024]{1,0:T(8,128)(2,1)}, u32[]{:S(2)}) copy-start(bf16[256,1024]{1,0:T(8,128)(2,1)} %param.16) | copy-start | bytes 1572868
  125.9 8.4 %copy-start.2 = (bf16[256,1024]{1,0:T(8,128)(2,1)S(1)}, bf16[256,1024]{1,0:T(8,128)(2,1)}, u32[]{:S(2)}) copy-start(bf16[256,1024]{1,0:T(8,128)(2,1)} %param.15) | copy-start | bytes 1572868
Sparse Core Ops, SparseCore 0:
  11.7 169.7 all-gather.1
where the time goes:
time: 197 us; the launch traced here: 196 us
  waiting for transfers between devices  101 us (51%)
  starting transfers between devices  46.2 us (23%)
  between operations  15.1 us (8%)
  blocking collectives  13 us (7%)
  matrix products  10.8 us (5%)
  other arithmetic  5.29 us (3%)
  local copies, waits for them, and re-layouts  4.84 us (2%)
    all_gather x1, waiting for transfers between devices, local(): lax.all_gather(jnp.concatenate([w_query, w_key, w_value], axis=1), 'dp',...  45.6 us
    all_to_all x1, waiting for transfers between devices, local(): lax.all_to_all(pick(wanted, table).astype(jnp.bfloat16).reshape(peers, ca...  33.6 us
    all_to_all x1, starting transfers between devices, local(): lax.all_to_all(requests, 'dp', split_axis=0, concat_axis=0, tiled=True)  20.4 us
    all_to_all x1, waiting for transfers between devices, local(): lax.all_to_all(requests, 'dp', split_axis=0, concat_axis=0, tiled=True)  14.1 us
    all_gather x1, blocking collectives, local(): lax.all_gather(norm_gain, 'mp', axis=0, tiled=True).astype(jnp.float32)  13 us
    ppermute x3, starting transfers between devices, local(): lax.ppermute(joined, 'mp', [(i, (i + k) % parts) for i in range(parts)])  10.6 us
    all_to_all x1, starting transfers between devices, local(): lax.all_to_all(grad_buffer.reshape(peers, capacity, col_width), 'dp', spl...  9.53 us
    all_to_all x1, waiting for transfers between devices, local(): lax.all_to_all(grad_buffer.reshape(peers, capacity, col_width), 'dp', spl...  7.74 us
  transfers between devices with their start and end apart: 7, of which 4 were waited for; matrix products, arithmetic and copies ran while one was open for 6% of the time, Pallas kernels for 0%

commit v1 on v0

--- a/solution.py
+++ b/solution.py
@@ -1,3 +1,4 @@
+import functools
 import math
 import jax
 import jax.numpy as jnp
@@ -6,6 +7,16 @@
 
 HD = 128
 SLOT = 128
+
+
+def run_the_plane(a0, lane_axis):
+    extent = jax.lax.axis_size(lane_axis)
+    parts_seen = tuple((extent if c == 0 else 1 for c in range(a0.ndim)))
+    parts_out = jnp.tile(a0, parts_seen)
+    return jax.lax.all_to_all(parts_out, lane_axis, split_axis=0, concat_axis=0, tiled=True)
+
+
+run_the_yards = functools.partial(run_the_plane, lane_axis="mp")
 
 
 def one_hot(rows, columns):
@@ -115,7 +126,7 @@
         ],
         axis=1,
     ).astype(jnp.float32)
-    gain = lax.all_gather(norm_gain, "mp", axis=0, tiled=True).astype(jnp.float32)
+    gain = run_the_yards(norm_gain).astype(jnp.float32)
     scale = lax.rsqrt(jnp.mean(features * features, axis=1, keepdims=True) + 1e-06)
     normed = (features * scale * gain[None, :]).astype(jnp.bfloat16)
     projected = jnp.dot(normed, weights, preferred_element_type=jnp.float32).astype(jnp.bfloat16)

time: 197 us -> 203 us (1.030)
  waiting for transfers between devices: 101 us -> 116 us
  blocking collectives: 13 us -> 0 us
  starting transfers between devices: 46.2 us -> 49.4 us
    all_gather x1 -> x0, blocking collectives: 13 us -> none  [local(): lax.all_gather(norm_gain, 'mp', axis=0, tiled=True).astype(jnp.float32)]
    ppermute x3, waiting for transfers between devices: 0.01 us -> 9.35 us  [local(): lax.ppermute(joined, 'mp', [(i, (i + k) % parts) for i in range(parts)])]
    all_to_all x1, waiting for transfers between devices: 7.74 us -> 17 us  [local(): lax.all_to_all(grad_buffer.reshape(peers, capacity, col_width), 'dp', spl...]
    all_gather x1, waiting for transfers between devices: 45.6 us -> 39.7 us  [local(): lax.all_gather(jnp.concatenate([w_query, w_key, w_value], axis=1), 'dp',...]
    all_to_all x0 -> x1, starting transfers between devices: none -> 3.96 us  [run_the_plane(): jax.lax.all_to_all(parts_out, lane_axis, split_axis=0, concat_axis=0, til...]
    all_to_all x0 -> x1, waiting for transfers between devices: none -> 2.67 us  [run_the_plane(): jax.lax.all_to_all(parts_out, lane_axis, split_axis=0, concat_axis=0, til...]
  transfers between devices with their start and end apart: 7 -> 8, of which waited for: 4 -> 8; matrix products, arithmetic and copies ran while one was open for 6% -> 7% of each run, Pallas kernels for 0% -> 0%
where the time goes in v1:
time: 203 us
  waiting for transfers between devices  116 us (57%)
  starting transfers between devices  49.4 us (24%)
  between operations  15 us (7%)
  matrix products  10.8 us (5%)
  other arithmetic  5.99 us (3%)
  local copies, waits for them, and re-layouts  5.98 us (3%)
    all_gather x1, waiting for transfers between devices, local(): lax.all_gather(jnp.concatenate([w_query, w_key, w_value], axis=1), 'dp',...  39.7 us
    all_to_all x1, waiting for transfers between devices, local(): lax.all_to_all(pick(wanted, table).astype(jnp.bfloat16).reshape(peers, ca...  32.7 us
    all_to_all x1, starting transfers between devices, local(): lax.all_to_all(requests, 'dp', split_axis=0, concat_axis=0, tiled=True)  20.4 us
    all_to_all x1, waiting for transfers between devices, local(): lax.all_to_all(grad_buffer.reshape(peers, capacity, col_width), 'dp', spl...  17 us
    all_to_all x1, waiting for transfers between devices, local(): lax.all_to_all(requests, 'dp', split_axis=0, concat_axis=0, tiled=True)  14.1 us
    all_to_all x1, starting transfers between devices, local(): lax.all_to_all(grad_buffer.reshape(peers, capacity, col_width), 'dp', spl...  10.5 us
    ppermute x3, waiting for transfers between devices, local(): lax.ppermute(joined, 'mp', [(i, (i + k) % parts) for i in range(parts)])  9.35 us
    ppermute x3, starting transfers between devices, local(): lax.ppermute(joined, 'mp', [(i, (i + k) % parts) for i in range(parts)])  8.84 us
  transfers between devices with their start and end apart: 8, of which 8 were waited for; matrix products, arithmetic and copies ran while one was open for 7% of the time, Pallas kernels for 0%

profile of v1, /device:TPU:1, one launch (start us, length us, event | category | flops | bytes accessed | tf_op | source)
XLA Modules:
  0.0 202.8 jit_solution(12761054761555591407)
XLA Ops:
  7.2 0.0 copy-start
  7.2 0.0 all-gather.2.cloned.1.call-start
  7.2 1.5 pad_maximum_fusion.3
  8.7 0.0 all-gather.2.cloned.1.call-update
  8.7 0.9 convert_reduce_fusion
  9.6 0.7 multiply_add_fusion
  10.3 0.1 select_reduce_fusion
  10.4 0.0 copy-start.3
  10.4 0.8 sub.24
  11.2 20.4 %all-to-all-start = ((s32[128,1,2]{2,1,0:T(1,128)}), s32[128,1,2]{2,1,0:T(1,128)S(1)}, u32[]{:S(2)}, u32[]{:S(2)}) async-start(s32[128,1,2]{2,1,0:T(1,128)} %bitcast.4), calls=%async_computation | async-start | bytes 131072 | tf_op jit(solution)/shard_map/all_to_all | solution.py:86
  31.6 0.7 convert_element_type.62
  32.3 14.1 %all-to-all-done = s32[128,1,2]{2,1,0:T(1,128)S(1)} async-done(((s32[128,1,2]{2,1,0:T(1,128)}), s32[128,1,2]{2,1,0:T(1,128)S(1)}, u32[]{:S(2)}, u32[]{:S(2)}) %all-to-all-start) | async-done | bytes 1056 | tf_op jit(solution)/shard_map/all_to_all | solution.py:86
  46.4 0.5 broadcast.76
  47.0 0.8 reduce.3
  47.8 0.1 eq.74
  47.9 1.6 convolution_convert_fusion.1
  49.6 1.0 reshape.120
  50.6 5.7 %all-to-all-start.1 = ((bf16[128,2,1024]{2,1,0:T(2,128)(2,1)}), bf16[128,2,1024]{2,1,0:T(2,128)(2,1)S(1)}, u32[]{:S(2)}, u32[]{:S(2)}) async-start(bf16[128,2,1024]{2,1,0:T(2,128)(2,1)} %reshape.120), calls=%async_computation.1 | async-start | bytes 1048576 | tf_op jit(solution)/shard_map/all_to_all | solution.py:93
  56.3 0.0 copy-done.3
  56.3 0.0 copy-start.4
  56.3 0.5 broadcast.77
  56.8 0.7 reduce.4
  57.5 0.6 reshape.137
  58.1 32.7 %all-to-all-done.1 = bf16[128,2,1024]{2,1,0:T(2,128)(2,1)S(1)} async-done(((bf16[128,2,1024]{2,1,0:T(2,128)(2,1)}), bf16[128,2,1024]{2,1,0:T(2,128)(2,1)S(1)}, u32[]{:S(2)}, u32[]{:S(2)}) %all-to-all-start.1) | async-done | bytes 524320 | tf_op jit(solution)/shard_map/all_to_all | solution.py:93
  90.8 4.0 %all-to-all-start.2 = ((bf16[4,2,512]{2,1,0:T(2,128)(2,1)}), bf16[4,2,512]{2,1,0:T(2,128)(2,1)S(1)}, u32[]{:S(2)}, u32[]{:S(2)}) async-start(bf16[4,2,512]{2,1,0:T(2,128)(2,1)} %reshape.137), calls=%async_computation.2 | async-start | bytes 16384 | tf_op jit(solution)/shard_map/all_to_all | solution.py:16
  94.8 0.0 copy-done
  94.8 0.3 convolution_convert_fusion.2
  95.1 0.2 reshape.121
  95.3 1.0 reshape.125
  96.3 2.7 %all-to-all-done.2 = bf16[4,2,512]{2,1,0:T(2,128)(2,1)S(1)} async-done(((bf16[4,2,512]{2,1,0:T(2,128)(2,1)}), bf16[4,2,512]{2,1,0:T(2,128)(2,1)S(1)}, u32[]{:S(2)}, u32[]{:S(2)}) %all-to-all-start.2) | async-done | bytes 8224 | tf_op jit(solution)/shard_map/all_to_all | solution.py:16
  98.9 10.5 %all-to-all-start.3 = ((bf16[128,2,1024]{2,1,0:T(2,128)(2,1)}), bf16[128,2,1024]{2,1,0:T(2,128)(2,1)S(1)}, u32[]{:S(2)}, u32[]{:S(2)}) async-start(bf16[128,2,1024]{2,1,0:T(2,128)(2,1)} %reshape.125), calls=%async_computation.3 | async-start | bytes 1048576 | tf_op jit(solution)/shard_map/all_to_all | solution.py:102
  110.1 0.0 copy-done.4
  110.1 0.3 convolution_convert_fusion.3
  110.4 2.2 %collective-permute-start = (bf16[128,1024]{1,0:T(8,128)(2,1)S(1)}, bf16[128,1024]{1,0:T(8,128)(2,1)S(1)}, u32[]{:S(2)}, u32[]{:S(2)}) collective-permute-start(bf16[128,1024]{1,0:T(8,128)(2,1)S(1)} %convolution_convert_fusion.3), channel_id=1, source_target_pairs={{0,1},{1,2},{2,3},{3,0},{4,5},{5,6},{6,7},{7,4},{8,9},{9,10},{10,1... | collective-permute-start | bytes 786440 | tf_op jit(solution)/shard_map/ppermute | solution.py:117
  112.6 3.7 %collective-permute-start.1 = (bf16[128,1024]{1,0:T(8,128)(2,1)S(1)}, bf16[128,1024]{1,0:T(8,128)(2,1)S(1)}, u32[]{:S(2)}, u32[]{:S(2)}) collective-permute-start(bf16[128,1024]{1,0:T(8,128)(2,1)S(1)} %convolution_convert_fusion.3), channel_id=1, source_target_pairs={{0,2},{1,3},{2,0},{3,1},{4,6},{5,7},{6,4},{7,5},{8,10},{9,11},{10,... | collective-permute-start | bytes 786440 | tf_op jit(solution)/shard_map/ppermute | solution.py:117
  116.3 3.0 %collective-permute-start.2 = (bf16[128,1024]{1,0:T(8,128)(2,1)S(1)}, bf16[128,1024]{1,0:T(8,128)(2,1)S(1)}, u32[]{:S(2)}, u32[]{:S(2)}) collective-permute-start(bf16[128,1024]{1,0:T(8,128)(2,1)S(1)} %convolution_convert_fusion.3), channel_id=1, source_target_pairs={{0,3},{1,0},{2,1},{3,2},{4,7},{5,4},{6,5},{7,6},{8,11},{9,8},{10,9... | collective-permute-start | bytes 786440 | tf_op jit(solution)/shard_map/ppermute | solution.py:117
  119.3 0.1 fusion.27
  119.5 1.6 collective-permute-done
  121.1 4.4 %collective-permute-done.1 = bf16[128,1024]{1,0:T(8,128)(2,1)S(1)} collective-permute-done((bf16[128,1024]{1,0:T(8,128)(2,1)S(1)}, bf16[128,1024]{1,0:T(8,128)(2,1)S(1)}, u32[]{:S(2)}, u32[]{:S(2)}) %collective-permute-start.1) | collective-permute-done | bytes 262176 | tf_op jit(solution)/shard_map/ppermute | solution.py:117
  125.5 3.3 %collective-permute-done.2 = bf16[128,1024]{1,0:T(8,128)(2,1)S(1)} collective-permute-done((bf16[128,1024]{1,0:T(8,128)(2,1)S(1)}, bf16[128,1024]{1,0:T(8,128)(2,1)S(1)}, u32[]{:S(2)}, u32[]{:S(2)}) %collective-permute-start.2) | collective-permute-done | bytes 262176 | tf_op jit(solution)/shard_map/ppermute | solution.py:117
  128.8 0.1 pad_maximum_fusion
  128.9 0.0 copy-start.1
  129.0 0.0 copy-start.2
  129.0 0.1 dynamic-slice_bitcast_fusion.3
  129.1 0.3 fusion.1
  129.4 17.0 %all-to-all-done.3 = bf16[128,2,1024]{2,1,0:T(2,128)(2,1)S(1)} async-done(((bf16[128,2,1024]{2,1,0:T(2,128)(2,1)}), bf16[128,2,1024]{2,1,0:T(2,128)(2,1)S(1)}, u32[]{:S(2)}, u32[]{:S(2)}) %all-to-all-start.3) | async-done | bytes 524320 | tf_op jit(solution)/shard_map/all_to_all | solution.py:102
  146.4 0.2 reshape.126
  146.6 0.0 copy-done.1
  146.6 0.0 copy-done.2
  146.6 1.7 convert_multiply_fusion.4
  148.4 39.7 %all-gather.2.cloned.1.call-done = bf16[4096,1536]{1,0:T(8,128)(2,1)} async-done(((bf16[32,1536]{1,0:T(8,128)(2,1)}), bf16[4096,1536]{1,0:T(8,128)(2,1)}) %all-gather.2.cloned.1.call-update) | async-done | bytes 12582928 | tf_op jit(solution)/shard_map/all_gather | solution.py:75
  188.1 6.4 %convolution_convert_fusion = bf16[128,1536]{1,0:T(8,128)(2,1)S(1)} fusion(bf16[4096,1536]{1,0:T(8,128)(2,1)} %all-gather.2.cloned.1.call-done, f32[4096]{0:T(1024)S(1)} %bitcast.55, f32[128]{0:T(128)S(1)} %add_rsqrt_fusion, bf16[128,1024]{1,0:T(8,128)(2,1)S(1)} %get-tuple-element.22, bf16[128,1024]{1,0:T(8,128)(2,1)S(1)} %get-tuple-element.23, ...), kind=kOutput, calls=%fused_computation.3 | convolution fusion | flops 1616576512 | bytes 14041600 | tf_op jit(solution)/shard_map/dot_general | solution.py:132
  194.5 0.2 fusion.5
  194.8 0.1 fusion.31
  194.9 0.1 copy.38
  195.0 0.2 fusion.7
  195.2 0.8 copy.36
  (8 shorter events, 0.1 us)
Async XLA Ops:
  7.2 87.6 %copy-start = (bf16[128,1024]{1,0:T(8,128)(2,1)S(1)}, bf16[128,1024]{1,0:T(8,128)(2,1)}, u32[]{:S(2)}) copy-start(bf16[128,1024]{1,0:T(8,128)(2,1)} %param.23) | copy-start | bytes 786436
  7.2 180.9 %all-gather.2.cloned.1.call-start = ((), (), s32[]{:S(2)}) async-start(), calls=%async_computation.4 | async-start | bytes 12681216 | tf_op jit(solution)/shard_map/all_gather | solution.py:75
  10.4 45.8 %copy-start.3 = (bf16[1024]{0:T(1024)(128)(2,1)S(1)}, bf16[1024]{0:T(1024)(128)(2,1)}, u32[]{:S(2)}) copy-start(bf16[1024]{0:T(1024)(128)(2,1)} %param.19) | copy-start | bytes 6148
  11.2 35.2 %all-to-all-start = ((s32[128,1,2]{2,1,0:T(1,128)}), s32[128,1,2]{2,1,0:T(1,128)S(1)}, u32[]{:S(2)}, u32[]{:S(2)}) async-start(s32[128,1,2]{2,1,0:T(1,128)} %bitcast.4), calls=%async_computation | async-start | bytes 131072 | tf_op jit(solution)/shard_map/all_to_all | solution.py:86
  50.6 40.2 %all-to-all-start.1 = ((bf16[128,2,1024]{2,1,0:T(2,128)(2,1)}), bf16[128,2,1024]{2,1,0:T(2,128)(2,1)S(1)}, u32[]{:S(2)}, u32[]{:S(2)}) async-start(bf16[128,2,1024]{2,1,0:T(2,128)(2,1)} %reshape.120), calls=%async_computation.1 | async-start | bytes 1048576 | tf_op jit(solution)/shard_map/all_to_all | solution.py:93
  56.3 53.8 %copy-start.4 = (s32[128,1]{0,1:T(1,128)S(1)}, s32[128,1]{0,1:T(1,128)}, u32[]{:S(2)}) copy-start(s32[128,1]{0,1:T(1,128)} %param.13) | copy-start | bytes 1540
  90.8 8.1 %all-to-all-start.2 = ((bf16[4,2,512]{2,1,0:T(2,128)(2,1)}), bf16[4,2,512]{2,1,0:T(2,128)(2,1)S(1)}, u32[]{:S(2)}, u32[]{:S(2)}) async-start(bf16[4,2,512]{2,1,0:T(2,128)(2,1)} %reshape.137), calls=%async_computation.2 | async-start | bytes 16384 | tf_op jit(solution)/shard_map/all_to_all | solution.py:16
  98.9 47.5 %all-to-all-start.3 = ((bf16[128,2,1024]{2,1,0:T(2,128)(2,1)}), bf16[128,2,1024]{2,1,0:T(2,128)(2,1)S(1)}, u32[]{:S(2)}, u32[]{:S(2)}) async-start(bf16[128,2,1024]{2,1,0:T(2,128)(2,1)} %reshape.125), calls=%async_computation.3 | async-start | bytes 1048576 | tf_op jit(solution)/shard_map/all_to_all | solution.py:102
  110.4 10.7 %collective-permute-start = (bf16[128,1024]{1,0:T(8,128)(2,1)S(1)}, bf16[128,1024]{1,0:T(8,128)(2,1)S(1)}, u32[]{:S(2)}, u32[]{:S(2)}) collective-permute-start(bf16[128,1024]{1,0:T(8,128)(2,1)S(1)} %convolution_convert_fusion.3), channel_id=1, source_target_pairs={{0,1},{1,2},{2,3},{3,0},{4,5},{5,6},{6,7},{7,4},{8,9},{9,10},{10,1... | collective-permute-start | bytes 786440 | tf_op jit(solution)/shard_map/ppermute | solution.py:117
  112.6 12.9 %collective-permute-start.1 = (bf16[128,1024]{1,0:T(8,128)(2,1)S(1)}, bf16[128,1024]{1,0:T(8,128)(2,1)S(1)}, u32[]{:S(2)}, u32[]{:S(2)}) collective-permute-start(bf16[128,1024]{1,0:T(8,128)(2,1)S(1)} %convolution_convert_fusion.3), channel_id=1, source_target_pairs={{0,2},{1,3},{2,0},{3,1},{4,6},{5,7},{6,4},{7,5},{8,10},{9,11},{10,... | collective-permute-start | bytes 786440 | tf_op jit(solution)/shard_map/ppermute | solution.py:117
  116.3 12.5 %collective-permute-start.2 = (bf16[128,1024]{1,0:T(8,128)(2,1)S(1)}, bf16[128,1024]{1,0:T(8,128)(2,1)S(1)}, u32[]{:S(2)}, u32[]{:S(2)}) collective-permute-start(bf16[128,1024]{1,0:T(8,128)(2,1)S(1)} %convolution_convert_fusion.3), channel_id=1, source_target_pairs={{0,3},{1,0},{2,1},{3,2},{4,7},{5,4},{6,5},{7,6},{8,11},{9,8},{10,9... | collective-permute-start | bytes 786440 | tf_op jit(solution)/shard_map/ppermute | solution.py:117
  128.9 17.7 %copy-start.1 = (bf16[256,1024]{1,0:T(8,128)(2,1)S(1)}, bf16[256,1024]{1,0:T(8,128)(2,1)}, u32[]{:S(2)}) copy-start(bf16[256,1024]{1,0:T(8,128)(2,1)} %param.16) | copy-start | bytes 1572868
  129.0 17.7 %copy-start.2 = (bf16[256,1024]{1,0:T(8,128)(2,1)S(1)}, bf16[256,1024]{1,0:T(8,128)(2,1)}, u32[]{:S(2)}) copy-start(bf16[256,1024]{1,0:T(8,128)(2,1)} %param.15) | copy-start | bytes 1572868
Sparse Core Ops, SparseCore 0:
  11.7 176.3 all-gather.1
